TPU v7x, 32 devices: a whole 2x2x4 slice. The times are simulated.
32 devices in a mesh: bl: 4 (over y, x), freq: 8 (over z, core).
Axes of the slice: x: 2, y: 2, z: 4, core: 2. Of those that a mesh axis runs over, the one named last changes fastest.
Arguments:
- visibilities: float32 [2, 2, 128, 8192], P(None, None, 'freq', 'bl'), may hold values from -8 to 8
- sample_flag_weight: int32 [2, 128, 8192], P(None, 'freq', 'bl'), may hold values from 0 to 4
- baseline_station_pair: int32 [2, 8192], P(None, 'bl'), may hold values from 0 to 511, as said below
- baseline_spatial_coords: float32 [2, 2, 8192], P(None, None, 'bl'), may hold values from -6 to 6
- directions: float32 [2, 8], replicated, may hold values from -0.5 to 0.5
- source_flux: float32 [8, 128], P(None, 'freq'), may hold values from 0.5 to 2
- channel_ratio: float32 [128], P('freq'), may hold values from 0.7 to 1.4
- jones_gains: float32 [2, 8, 128, 512], P(None, None, 'freq'), may hold values from -4 to 4
- scaled_dual: float32 [2, 8, 128, 512], P(None, None, 'freq'), may hold values from -2 to 2
- consensus: float32 [2, 3, 8, 512], replicated, may hold values from -3 to 3
- penalty: float32 [8], replicated, may hold values from 0.3 to 3
Outputs:
- new_gains: float32 [2, 8, 128, 512], P(None, None, 'freq')
- new_consensus: float32 [2, 3, 8, 512], replicated
- new_dual: float32 [2, 8, 128, 512], P(None, None, 'freq')
- residuals: float32 [2, 2, 128, 8192], P(None, None, 'freq', 'bl')
Inputs may be any that keep to these rules, and one draw needn't show every extreme that they name: `baseline_station_pair`: the two stations of every baseline differ.
All inputs are finite; a program needn't handle non-finite values.
Results may differ from a plain program's by a relative error of at most 0.00016.
Values sent between devices are 32-bit elements; how exact they have to be, the bound alone decides.
A program may use at most 64 MiB of HBM per device.

v0:
```python
import math
import jax
import jax.numpy as jnp
from jax import lax
from jax.sharding import PartitionSpec as P

NPOLY = 3
ITERS = 3
robust_dof = 2.0
small_term = 1e-06
two_pi = 2.0 * math.pi


def legendre(ratios):
    scaled = (ratios - 1.05) / 0.35
    values = [jnp.ones_like(scaled), scaled]
    values.append((3 * scaled * values[1] - 1 * values[0]) / 2)
    return jnp.stack(values[:NPOLY])


def coherency(coords, sky_dirs, fluxes, ratios):
    project = (
        sky_dirs[0][:, None, None] * coords[0][None] + sky_dirs[1][:, None, None] * coords[1][None]
    )
    phases = two_pi * project[:, :, None, :] * ratios[None, None, :, None]
    amplitude = fluxes[:, None, :, None]
    return (amplitude * jnp.cos(phases), amplitude * jnp.sin(phases))


def station_table(pair_row, station_list):
    positions = lax.broadcasted_iota(jnp.int32, (station_list, pair_row.shape[0]), 0)
    return (positions == pair_row[None, :]).astype(jnp.float32)


def pick_stations(gain_re, gain_im, table):
    stacked = jnp.stack([gain_re, gain_im])
    lead_shape = stacked.shape[:3]
    flat = stacked.reshape(-1, stacked.shape[3])
    picked = jnp.dot(
        flat, table, precision=lax.Precision.HIGHEST, preferred_element_type=jnp.float32
    )
    picked = picked.reshape(lead_shape + (table.shape[1],))
    return (picked[0], picked[1])


def predict(gain_re, gain_im, left_table, right_table, sky_re, sky_im):
    left_re, left_im = pick_stations(gain_re, gain_im, left_table)
    right_re, right_im = pick_stations(gain_re, gain_im, right_table)
    pair_re = left_re * right_re + left_im * right_im
    pair_im = left_im * right_re - left_re * right_im
    model_re = pair_re[:, None] * sky_re - pair_im[:, None] * sky_im
    model_im = pair_re[:, None] * sky_im + pair_im[:, None] * sky_re
    return ((left_re, left_im, right_re, right_im), model_re, model_im)


def residual_of(observed, model_re, model_im):
    return (observed[0] - jnp.sum(model_re, axis=0), observed[1] - jnp.sum(model_im, axis=0))


def robust_weights(flagged, error_re, error_im, sigma_sq):
    return (
        flagged
        * (robust_dof + 1.0)
        / (robust_dof + (error_re * error_re + error_im * error_im) / sigma_sq)
    )


def normal_terms(
    error_re,
    error_im,
    model_re,
    model_im,
    weights,
    sky_re,
    sky_im,
    side_gains,
    left_table,
    right_table,
):
    target_re = error_re[None] + model_re
    target_im = error_im[None] + model_im
    cross_re = sky_re * target_re + sky_im * target_im
    cross_im = sky_re * target_im - sky_im * target_re
    weight_wide = weights[None]
    summed_re = jnp.sum(weight_wide * cross_re, axis=1)
    summed_im = jnp.sum(weight_wide * cross_im, axis=1)
    powers = jnp.sum(weight_wide * (sky_re * sky_re + sky_im * sky_im), axis=1)
    left_re, left_im, right_re, right_im = side_gains
    first_re = right_re * summed_re - right_im * summed_im
    first_im = right_re * summed_im + right_im * summed_re
    second_re = left_re * summed_re + left_im * summed_im
    second_im = left_im * summed_re - left_re * summed_im
    first_norm = (right_re * right_re + right_im * right_im) * powers
    second_norm = (left_re * left_re + left_im * left_im) * powers
    stacked_first = jnp.stack([first_re, first_im, first_norm])
    stacked_second = jnp.stack([second_re, second_im, second_norm])
    lead_shape = stacked_first.shape[:3]
    baseline_count = stacked_first.shape[3]
    contract = (((1,), (1,)), ((), ()))
    into_first = lax.dot_general(
        stacked_first.reshape(-1, baseline_count),
        left_table,
        contract,
        precision=lax.Precision.HIGHEST,
        preferred_element_type=jnp.float32,
    )
    into_second = lax.dot_general(
        stacked_second.reshape(-1, baseline_count),
        right_table,
        contract,
        precision=lax.Precision.HIGHEST,
        preferred_element_type=jnp.float32,
    )
    return (into_first + into_second).reshape(lead_shape + (left_table.shape[0],))


def update_gains(gain_re, gain_im, normal_sums, anchor_re, anchor_im, effective_penalty):
    penalty_wide = effective_penalty[:, None, None]
    divisor = normal_sums[2] + penalty_wide
    solved_re = (normal_sums[0] + penalty_wide * anchor_re) / divisor
    solved_im = (normal_sums[1] + penalty_wide * anchor_im) / divisor
    return (0.5 * (gain_re + solved_re), 0.5 * (gain_im + solved_im))


def cholesky_solve(gram_total, flat_rhs):
    factor = jnp.linalg.cholesky(gram_total)
    matrix_order = gram_total.shape[0]
    forward = []
    for row_index in range(matrix_order):
        running = flat_rhs[row_index]
        for col_index in range(row_index):
            running = running - factor[row_index, col_index] * forward[col_index]
        forward.append(running / factor[row_index, row_index])
    backward = [None] * matrix_order
    for row_index in reversed(range(matrix_order)):
        running = forward[row_index]
        for col_index in range(row_index + 1, matrix_order):
            running = running - factor[col_index, row_index] * backward[col_index]
        backward[row_index] = running / factor[row_index, row_index]
    return jnp.stack(backward)


def solve_consensus(gram_total, rhs_total):
    matrix_order = gram_total.shape[0]
    flat_rhs = jnp.moveaxis(rhs_total, 1, 0).reshape(matrix_order, -1)
    solved = cholesky_solve(gram_total, flat_rhs)
    return jnp.moveaxis(
        solved.reshape((matrix_order, rhs_total.shape[0]) + rhs_total.shape[2:]), 0, 1
    )


def body(
    visibilities,
    sample_flag_weight,
    baseline_station_pair,
    baseline_spatial_coords,
    directions,
    source_flux,
    channel_ratio,
    jones_gains,
    scaled_dual,
    consensus,
    penalty,
):
    station_list = jones_gains.shape[3]
    baseline_list = baseline_station_pair.shape[1] * lax.axis_size("bl")
    solution_time_slots = visibilities.shape[1]
    effective_penalty = penalty * (2.0 * baseline_list * solution_time_slots / station_list)
    left_table = station_table(baseline_station_pair[0], station_list)
    right_table = station_table(baseline_station_pair[1], station_list)
    sky_re, sky_im = coherency(baseline_spatial_coords, directions, source_flux, channel_ratio)
    poly_basis = legendre(channel_ratio)
    gram_local = jnp.dot(poly_basis, poly_basis.T, precision=lax.Precision.HIGHEST)
    anchor = (
        jnp.einsum("jc,xjks->xkcs", poly_basis, consensus, precision=lax.Precision.HIGHEST)
        - scaled_dual
    )
    anchor_re, anchor_im = (anchor[0], anchor[1])
    flagged = sample_flag_weight.astype(jnp.float32)
    count_local = jnp.sum(flagged)
    gain_re, gain_im = (jones_gains[0], jones_gains[1])
    for iteration in range(ITERS):
        side_gains, model_re, model_im = predict(
            gain_re, gain_im, left_table, right_table, sky_re, sky_im
        )
        error_re, error_im = residual_of(visibilities, model_re, model_im)
        misfit_local = jnp.sum(flagged * (error_re * error_re + error_im * error_im))
        squares, weight_total = lax.psum((misfit_local, count_local), ("bl", "freq"))
        sigma_sq = squares / (weight_total + 1.0) + small_term
        weights = robust_weights(flagged, error_re, error_im, sigma_sq)
        partial_value = normal_terms(
            error_re,
            error_im,
            model_re,
            model_im,
            weights,
            sky_re,
            sky_im,
            side_gains,
            left_table,
            right_table,
        )
        owned_sums = lax.psum_scatter(partial_value, "bl", scatter_dimension=3, tiled=True)
        own_width = owned_sums.shape[3]
        offset = lax.axis_index("bl") * own_width
        own_gain_re = lax.dynamic_slice_in_dim(gain_re, offset, own_width, 2)
        own_gain_im = lax.dynamic_slice_in_dim(gain_im, offset, own_width, 2)
        own_anchor_re = lax.dynamic_slice_in_dim(anchor_re, offset, own_width, 2)
        own_anchor_im = lax.dynamic_slice_in_dim(anchor_im, offset, own_width, 2)
        new_re, new_im = update_gains(
            own_gain_re, own_gain_im, owned_sums, own_anchor_re, own_anchor_im, effective_penalty
        )
        gathered = lax.all_gather(jnp.stack([new_re, new_im]), "bl", axis=3, tiled=True)
        gain_re, gain_im = (gathered[0], gathered[1])
    side_gains, model_re, model_im = predict(
        gain_re, gain_im, left_table, right_table, sky_re, sky_im
    )
    error_re, error_im = residual_of(visibilities, model_re, model_im)
    residuals = jnp.stack([error_re, error_im])
    new_gains = jnp.stack([gain_re, gain_im])
    rhs_local = jnp.einsum(
        "jc,xkcs->xjks", poly_basis, new_gains + scaled_dual, precision=lax.Precision.HIGHEST
    )
    rhs_total, gram_total = lax.psum((rhs_local, gram_local), "freq")
    new_consensus = solve_consensus(gram_total, rhs_total)
    new_dual = (
        scaled_dual
        + new_gains
        - jnp.einsum("jc,xjks->xkcs", poly_basis, new_consensus, precision=lax.Precision.HIGHEST)
    )
    return (new_gains, new_consensus, new_dual, residuals)


def solution(mesh):
    in_specs = (
        P(None, None, "freq", "bl"),
        P(None, "freq", "bl"),
        P(None, "bl"),
        P(None, None, "bl"),
        P(),
        P(None, "freq"),
        P("freq"),
        P(None, None, "freq", None),
        P(None, None, "freq", None),
        P(),
        P(),
    )
    out_specs = (
        P(None, None, "freq", None),
        P(),
        P(None, None, "freq", None),
        P(None, None, "freq", "bl"),
    )
    return jax.shard_map(body, mesh=mesh, in_specs=in_specs, out_specs=out_specs, check_vma=False)
```

profile of v0, /device:TPU:8, one launch (start us, length us, event | category | flops | bytes accessed | tf_op | source)
XLA Modules:
  0.0 447.2 jit_solution(5179471884949867166)
XLA Ops:
  16.0 9.0 %fusion.102 = (f32[2,16,2048]{2,1,0:T(8,128)S(1)}, f32[2,16,2048]{2,1,0:T(8,128)S(1)}) fusion(f32[8,16,2048]{2,1,0:T(8,128)S(1)} %bitcast.263, f32[16]{0:T(128)S(1)} %copy-done.28, f32[8,2,2048]{2,1,0:T(2,128)S(1)} %add_multiply_fusion, f32[8,16]{1,0:T(8,128)S(1)} %copy-done.26, f32[8,16,2048]{2,1,0:T(8,128)S(1)} %bitcast.261), kind=kLoop, calls=%fused_computation.115 | loop fusion | flops 5636096 | bytes 2753088 | tf_op jit(solution)/shard_map/reduce_sum | solution.py:57
  27.2 40.9 %all-reduce = (f32[]{:T(128)}, f32[]{:T(128)}) all-reduce(f32[]{:T(128)} %get-tuple-element.34, f32[]{:T(128)} %get-tuple-element.33), channel_id=1, replica_groups=mesh['bl'=4,'freq'=8] {'bl','freq'}, use_global_device_ids=true, to_apply=%region_3.0 | all-reduce | flops 2 | bytes 16 | tf_op jit(solution)/shard_map/psum | solution.py:188
  70.4 10.9 %fusion.36 = (f32[8,16,2048]{2,1,0:T(8,128)S(1)}, f32[8,16,2048]{2,1,0:T(8,128)S(1)}, f32[8,16,2048]{2,1,0:T(8,128)S(1)}) fusion(f32[2,16,2048]{2,1,0:T(8,128)} %get-tuple-element.104, f32[2,16,2048]{2,1,0:T(8,128)S(1)} %get-tuple-element.103, f32[2,16,2048]{2,1,0:T(8,128)S(1)} %add_divide_fusion.2, f32[8,16,2048]{2,1,0:T(8,128)S(1)} %bitcast.264, ...), kind=kLoop, calls=%fused_computation.46 | loop fusion | flops 12845056 | bytes 6160960 | tf_op jit(solution)/shard_map/reduce_sum | solution.py:85
  86.7 3.9 fusion.103
  92.5 24.4 %reduce-scatter.4.cloned.1.call-done = f32[3,8,16,128]{3,2,1,0:T(8,128)} async-done(((f32[3,8,16,512]{3,2,1,0:T(8,128)}), f32[3,8,16,128]{3,2,1,0:T(8,128)}) %reduce-scatter.4.cloned.1.call-update) | async-done | bytes 196624 | tf_op jit(solution)/shard_map/reduce_scatter | solution.py:203
  118.0 13.3 %all_gather.9 = f32[2,8,16,512]{3,2,1,0:T(8,128)S(1)} all-gather(f32[2,8,16,128]{3,2,1,0:T(8,128)S(1)} %pad_maximum_fusion.7), channel_id=1, replica_groups=mesh['bl'=4,'freq'=8] {'bl'}, dimensions={3}, use_global_device_ids=true | all-gather | bytes 655360 | tf_op jit(solution)/shard_map/all_gather | solution.py:213
  137.9 9.0 %fusion.98 = (f32[2,16,2048]{2,1,0:T(8,128)S(1)}, f32[2,16,2048]{2,1,0:T(8,128)S(1)}) fusion(f32[8,16,2048]{2,1,0:T(8,128)S(1)} %bitcast.271, f32[8,16,2048]{2,1,0:T(8,128)S(1)} %bitcast.269, f32[16]{0:T(128)S(1)} %copy-done.28, f32[8,2,2048]{2,1,0:T(2,128)S(1)} %add_multiply_fusion, f32[8,16]{1,0:T(8,128)S(1)} %copy-done.26), kind=kLoop, calls=%fused_computation.111 | loop fusion | flops 5636096 | bytes 2753088 | tf_op jit(solution)/shard_map/reduce_sum | solution.py:57
  149.1 39.8 %psum.50 = f32[]{:T(128)} all-reduce(f32[]{:T(128)} %get-tuple-element.42), channel_id=1, replica_groups=mesh['bl'=4,'freq'=8] {'bl','freq'}, use_global_device_ids=true, to_apply=%region_13.0 | all-reduce | flops 1 | bytes 8 | tf_op jit(solution)/shard_map/psum | solution.py:188
  190.5 10.9 %fusion.45 = (f32[8,16,2048]{2,1,0:T(8,128)S(1)}, f32[8,16,2048]{2,1,0:T(8,128)S(1)}, f32[8,16,2048]{2,1,0:T(8,128)S(1)}) fusion(f32[2,16,2048]{2,1,0:T(8,128)} %get-tuple-element.98, f32[2,16,2048]{2,1,0:T(8,128)S(1)} %get-tuple-element.97, f32[2,16,2048]{2,1,0:T(8,128)S(1)} %add_divide_fusion.1, f32[8,16,2048]{2,1,0:T(8,128)S(1)} %bitcast.272, ...), kind=kLoop, calls=%fused_computation.55 | loop fusion | flops 12845056 | bytes 6160960 | tf_op jit(solution)/shard_map/reduce_sum | solution.py:85
  206.6 3.9 fusion.104
  210.6 26.2 %reduce-scatter.6.cloned.1.call-done = f32[3,8,16,128]{3,2,1,0:T(8,128)} async-done(((f32[3,8,16,512]{3,2,1,0:T(8,128)}), f32[3,8,16,128]{3,2,1,0:T(8,128)}) %reduce-scatter.6.cloned.1.call-update) | async-done | bytes 196624 | tf_op jit(solution)/shard_map/reduce_scatter | solution.py:203
  237.9 13.5 %all_gather.10 = f32[2,8,16,512]{3,2,1,0:T(8,128)S(1)} all-gather(f32[2,8,16,128]{3,2,1,0:T(8,128)S(1)} %pad_maximum_fusion.8), channel_id=1, replica_groups=mesh['bl'=4,'freq'=8] {'bl'}, dimensions={3}, use_global_device_ids=true | all-gather | bytes 655360 | tf_op jit(solution)/shard_map/all_gather | solution.py:213
  258.0 9.0 %fusion.94 = (f32[2,16,2048]{2,1,0:T(8,128)S(1)}, f32[2,16,2048]{2,1,0:T(8,128)S(1)}) fusion(f32[8,16,2048]{2,1,0:T(8,128)S(1)} %bitcast.267, f32[8,16,2048]{2,1,0:T(8,128)S(1)} %bitcast.265, f32[16]{0:T(128)S(1)} %copy-done.28, f32[8,2,2048]{2,1,0:T(2,128)S(1)} %add_multiply_fusion, f32[8,16]{1,0:T(8,128)S(1)} %copy-done.26), kind=kLoop, calls=%fused_computation.107 | loop fusion | flops 5636096 | bytes 2753088 | tf_op jit(solution)/shard_map/reduce_sum | solution.py:57
  269.2 39.7 %psum.51 = f32[]{:T(128)} all-reduce(f32[]{:T(128)} %get-tuple-element.40), channel_id=1, replica_groups=mesh['bl'=4,'freq'=8] {'bl','freq'}, use_global_device_ids=true, to_apply=%region_21.0 | all-reduce | flops 1 | bytes 8 | tf_op jit(solution)/shard_map/psum | solution.py:188
  310.6 10.9 %fusion.53 = (f32[8,16,2048]{2,1,0:T(8,128)S(1)}, f32[8,16,2048]{2,1,0:T(8,128)S(1)}, f32[8,16,2048]{2,1,0:T(8,128)S(1)}) fusion(f32[2,16,2048]{2,1,0:T(8,128)} %get-tuple-element.94, f32[2,16,2048]{2,1,0:T(8,128)S(1)} %get-tuple-element.93, f32[2,16,2048]{2,1,0:T(8,128)S(1)} %add_divide_fusion, f32[8,16,2048]{2,1,0:T(8,128)S(1)} %bitcast.268, ...), kind=kLoop, calls=%fused_computation.63 | loop fusion | flops 12845056 | bytes 6160960 | tf_op jit(solution)/shard_map/reduce_sum | solution.py:85
  326.7 3.9 fusion.105
  330.9 11.1 %psum.53 = f32[3,3]{0,1:T(4,128)S(1)} all-reduce(f32[3,3]{0,1:T(4,128)S(1)} %fusion.163), channel_id=1, replica_groups=mesh['bl'=4,'freq'=8] {'freq'}, use_global_device_ids=true, to_apply=%region_27.0 | all-reduce | flops 9 | bytes 72 | tf_op jit(solution)/shard_map/psum | solution.py:224
  345.7 11.2 %reduce-scatter.8.cloned.1.call-done = f32[3,8,16,128]{3,2,1,0:T(8,128)} async-done(((f32[3,8,16,512]{3,2,1,0:T(8,128)}), f32[3,8,16,128]{3,2,1,0:T(8,128)}) %reduce-scatter.8.cloned.1.call-update) | async-done | bytes 196624 | tf_op jit(solution)/shard_map/reduce_scatter | solution.py:203
  358.0 13.3 %all_gather.11 = f32[2,8,16,512]{3,2,1,0:T(8,128)S(1)} all-gather(f32[2,8,16,128]{3,2,1,0:T(8,128)S(1)} %pad_maximum_fusion.9), channel_id=1, replica_groups=mesh['bl'=4,'freq'=8] {'bl'}, dimensions={3}, use_global_device_ids=true | all-gather | bytes 655360 | tf_op jit(solution)/shard_map/all_gather | solution.py:213
  371.3 3.4 fusion
  374.7 3.4 fusion.7
  381.9 8.9 %fusion.58 = (f32[2,16,2048]{2,1,0:T(8,128)S(1)}, f32[2,16,2048]{2,1,0:T(8,128)S(1)}) fusion(f32[8,16,2048]{2,1,0:T(8,128)S(1)} %bitcast.276, f32[8,16,2048]{2,1,0:T(8,128)S(1)} %bitcast.275, f32[16]{0:T(128)S(1)} %copy-done.28, f32[8,2,2048]{2,1,0:T(2,128)S(1)} %add_multiply_fusion, f32[8,16]{1,0:T(8,128)S(1)} %copy-done.26), kind=kLoop, calls=%fused_computation.68 | loop fusion | flops 5636096 | bytes 2753088 | tf_op jit(solution)/shard_map/reduce_sum | solution.py:57
  391.7 41.8 %all-reduce.3.cloned.1.call-done = f32[3,2,8,512]{3,2,1,0:T(8,128)} async-done(((f32[3,2,8,512]{3,2,1,0:T(8,128)}), f32[3,2,8,512]{3,2,1,0:T(8,128)}) %all-reduce.3.cloned.1.call-update) | async-done | bytes 98320 | tf_op jit(solution)/shard_map/psum | solution.py:224
  433.5 4.0 subtract_divide_fusion
  (135 shorter events, 62.5 us)
Async XLA Ops:
  7.2 83.7 %copy-start = (f32[2,3,8,512]{3,2,1,0:T(8,128)S(1)}, f32[2,3,8,512]{3,2,1,0:T(8,128)}, u32[]{:S(2)}) copy-start(f32[2,3,8,512]{3,2,1,0:T(8,128)} %param.20) | copy-start | bytes 294916
  7.2 109.8 %reduce-scatter.4.cloned.1.call-start = ((), (), s32[]{:S(2)}) async-start(), calls=%async_computation.3 | async-start | bytes 983040 | tf_op jit(solution)/shard_map/reduce_scatter | solution.py:203
  15.8 9.2 %copy-start.2 = (f32[2,2,16,2048]{3,2,1,0:T(8,128)S(1)}, f32[2,2,16,2048]{3,2,1,0:T(8,128)}, u32[]{:S(2)}) copy-start(f32[2,2,16,2048]{3,2,1,0:T(8,128)} %param.11) | copy-start | bytes 1572868
  16.0 9.8 %copy-start.3 = (s32[2,16,2048]{2,1,0:T(8,128)S(1)}, s32[2,16,2048]{2,1,0:T(8,128)}, u32[]{:S(2)}) copy-start(s32[2,16,2048]{2,1,0:T(8,128)} %param.12) | copy-start | bytes 786436
  70.4 10.9 %copy-start.4 = (f32[128,2048]{1,0:T(8,128)S(1)}, f32[128,2048]{1,0:T(8,128)}, u32[]{:S(2)}) copy-start(f32[128,2048]{1,0:T(8,128)} %get-tuple-element.85) | copy-start | bytes 3145732
  70.4 10.9 %copy-start.5 = (f32[128,2048]{1,0:T(8,128)S(1)}, f32[128,2048]{1,0:T(8,128)}, u32[]{:S(2)}) copy-start(f32[128,2048]{1,0:T(8,128)} %get-tuple-element.86) | copy-start | bytes 3145732
  70.4 10.9 %copy-start.6 = (f32[128,2048]{1,0:T(8,128)S(1)}, f32[128,2048]{1,0:T(8,128)}, u32[]{:S(2)}) copy-start(f32[128,2048]{1,0:T(8,128)} %get-tuple-element.87) | copy-start | bytes 3145732
  70.4 10.9 %copy-start.7 = (f32[128,2048]{1,0:T(8,128)S(1)}, f32[128,2048]{1,0:T(8,128)}, u32[]{:S(2)}) copy-start(f32[128,2048]{1,0:T(8,128)} %get-tuple-element.88) | copy-start | bytes 3145732
  86.7 4.1 copy-start.25
  90.7 146.1 %reduce-scatter.6.cloned.1.call-start = ((), (), s32[]{:S(2)}) async-start(), calls=%async_computation.4 | async-start | bytes 983040 | tf_op jit(solution)/shard_map/reduce_scatter | solution.py:203
  92.5 40.8 %copy-start.22 = (f32[1,8,16,512]{3,2,1,0:T(8,128)}, f32[1,8,16,512]{3,2,1,0:T(8,128)S(1)}, u32[]{:S(2)}) copy-start(f32[1,8,16,512]{3,2,1,0:T(8,128)S(1)} %get-tuple-element.99) | copy-start | bytes 786436
  92.5 40.8 %copy-start.23 = (f32[1,8,16,512]{3,2,1,0:T(8,128)}, f32[1,8,16,512]{3,2,1,0:T(8,128)S(1)}, u32[]{:S(2)}) copy-start(f32[1,8,16,512]{3,2,1,0:T(8,128)S(1)} %get-tuple-element.100) | copy-start | bytes 786436
  190.5 10.9 %copy-start.12 = (f32[128,2048]{1,0:T(8,128)S(1)}, f32[128,2048]{1,0:T(8,128)}, u32[]{:S(2)}) copy-start(f32[128,2048]{1,0:T(8,128)} %get-tuple-element.77) | copy-start | bytes 3145732
  190.5 10.9 %copy-start.13 = (f32[128,2048]{1,0:T(8,128)S(1)}, f32[128,2048]{1,0:T(8,128)}, u32[]{:S(2)}) copy-start(f32[128,2048]{1,0:T(8,128)} %get-tuple-element.78) | copy-start | bytes 3145732
  190.5 10.9 %copy-start.14 = (f32[128,2048]{1,0:T(8,128)S(1)}, f32[128,2048]{1,0:T(8,128)}, u32[]{:S(2)}) copy-start(f32[128,2048]{1,0:T(8,128)} %get-tuple-element.79) | copy-start | bytes 3145732
  190.5 10.9 %copy-start.15 = (f32[128,2048]{1,0:T(8,128)S(1)}, f32[128,2048]{1,0:T(8,128)}, u32[]{:S(2)}) copy-start(f32[128,2048]{1,0:T(8,128)} %get-tuple-element.80) | copy-start | bytes 3145732
  210.5 146.4 %reduce-scatter.8.cloned.1.call-start = ((), (), s32[]{:S(2)}) async-start(), calls=%async_computation.5 | async-start | bytes 983040 | tf_op jit(solution)/shard_map/reduce_scatter | solution.py:203
  310.6 10.9 %copy-start.8 = (f32[128,2048]{1,0:T(8,128)S(1)}, f32[128,2048]{1,0:T(8,128)}, u32[]{:S(2)}) copy-start(f32[128,2048]{1,0:T(8,128)} %get-tuple-element.69) | copy-start | bytes 3145732
  310.6 10.9 %copy-start.9 = (f32[128,2048]{1,0:T(8,128)S(1)}, f32[128,2048]{1,0:T(8,128)}, u32[]{:S(2)}) copy-start(f32[128,2048]{1,0:T(8,128)} %get-tuple-element.70) | copy-start | bytes 3145732
  310.6 10.9 %copy-start.10 = (f32[128,2048]{1,0:T(8,128)S(1)}, f32[128,2048]{1,0:T(8,128)}, u32[]{:S(2)}) copy-start(f32[128,2048]{1,0:T(8,128)} %get-tuple-element.71) | copy-start | bytes 3145732
  310.6 10.9 %copy-start.11 = (f32[128,2048]{1,0:T(8,128)S(1)}, f32[128,2048]{1,0:T(8,128)}, u32[]{:S(2)}) copy-start(f32[128,2048]{1,0:T(8,128)} %get-tuple-element.72) | copy-start | bytes 3145732
  326.7 19.0 %copy-start.19 = (f32[2,8,16,512]{3,2,1,0:T(8,128)S(1)}, f32[2,8,16,512]{3,2,1,0:T(8,128)}, u32[]{:S(2)}) copy-start(f32[2,8,16,512]{3,2,1,0:T(8,128)} %copy-done.18) | copy-start | bytes 1572868
  330.6 102.9 %all-reduce.3.cloned.1.call-start = ((), (), s32[]{:S(2)}) async-start(), calls=%async_computation.6 | async-start | bytes 196608 | tf_op jit(solution)/shard_map/psum | solution.py:224
  390.8 49.6 %copy-start.1 = (f32[2,3,8,512]{3,2,1,0:T(8,128)S(1)}, f32[2,3,8,512]{3,2,1,0:T(8,128)}, u32[]{:S(2)}) copy-start(f32[2,3,8,512]{3,2,1,0:T(8,128)} %param.20) | copy-start | bytes 294916
  (11 other events, 29.4 us)
Sparse Core Ops, SparseCore 0:
  90.8 26.0 reduce-scatter.3
  210.7 26.1 reduce-scatter.5
  330.7 26.1 reduce-scatter.7
  379.5 54.0 all-reduce.2
where the time goes:
time: 453 us; the launch traced here: 447 us
  blocking collectives  171 us (38%)
  other arithmetic  104 us (23%)
  waiting for transfers between devices  104 us (23%)
  matrix products  44.3 us (10%)
  between operations  18.7 us (4%)
  local copies, waits for them, and re-layouts  4.85 us (1%)
    psum x3, blocking collectives, body(): lax.psum((misfit_local, count_local), ('bl', 'freq'))  120 us
    reduce_scatter x3, waiting for transfers between devices, body(): lax.psum_scatter(partial_value, 'bl', scatter_dimension=3, tiled=True)  61.8 us
    psum x1, waiting for transfers between devices, body(): rhs_total, gram_total = lax.psum((rhs_local, gram_local), 'freq')  41.8 us
    all_gather x3, blocking collectives, body(): lax.all_gather(jnp.stack([new_re, new_im]), 'bl', axis=3, tiled=True)  40 us
    reduce_sum x4, other arithmetic, residual_of(): jnp.sum(model_re, axis=0)  35.9 us
    reduce_sum x3, other arithmetic, normal_terms(): summed_re = jnp.sum(weight_wide * cross_re, axis=1)  32.6 us
    dot_general x8, matrix products, pick_stations(): jnp.dot(flat, table, precision=lax.Precision.HIGHEST, preferred_element_t...  20.6 us
    dot_general x3, matrix products, normal_terms(): lax.dot_general(stacked_second.reshape(-1, baseline_count), right_table,...  11.8 us
  transfers between devices with their start and end apart: 4, of which 4 were waited for; matrix products, arithmetic and copies ran while one was open for 4% of the time, Pallas kernels for 0%

commit v1 on v0

--- a/solution.py
+++ b/solution.py
@@ -185,7 +185,7 @@
         )
         error_re, error_im = residual_of(visibilities, model_re, model_im)
         misfit_local = jnp.sum(flagged * (error_re * error_re + error_im * error_im))
-        squares, weight_total = lax.psum((misfit_local, count_local), ("bl", "freq"))
+        squares, weight_total = lax.psum(lax.psum((misfit_local, count_local), "bl"), "freq")
         sigma_sq = squares / (weight_total + 1.0) + small_term
         weights = robust_weights(flagged, error_re, error_im, sigma_sq)
         partial_value = normal_terms(

time: 453 us -> 399 us (0.88)
  blocking collectives: 171 us -> 103 us
  waiting for transfers between devices: 104 us -> 115 us
    psum x4 -> x6, blocking collectives: 131 us -> 63.2 us  [the longest x3 33.6 us: body(): lax.psum(lax.psum((misfit_local, count_local), 'bl'), 'freq')]
    reduce_scatter x3, waiting for transfers between devices: 61.8 us -> 73.4 us  [body(): lax.psum_scatter(partial_value, 'bl', scatter_dimension=3, tiled=True)]
where the time goes in v1:
time: 399 us; the launch traced here: 393 us
  waiting for transfers between devices  115 us (29%)
  other arithmetic  106 us (27%)
  blocking collectives  103 us (26%)
  matrix products  44.3 us (11%)
  between operations  18.7 us (5%)
  local copies, waits for them, and re-layouts  5.56 us (1%)
    reduce_scatter x3, waiting for transfers between devices, body(): lax.psum_scatter(partial_value, 'bl', scatter_dimension=3, tiled=True)  73.4 us
    psum x1, waiting for transfers between devices, body(): rhs_total, gram_total = lax.psum((rhs_local, gram_local), 'freq')  41.7 us
    all_gather x3, blocking collectives, body(): lax.all_gather(jnp.stack([new_re, new_im]), 'bl', axis=3, tiled=True)  40 us
    reduce_sum x4, other arithmetic, residual_of(): jnp.sum(model_re, axis=0)  35.8 us
    psum x3, blocking collectives, body(): lax.psum(lax.psum((misfit_local, count_local), 'bl'), 'freq')  33.6 us
    reduce_sum x3, other arithmetic, normal_terms(): summed_re = jnp.sum(weight_wide * cross_re, axis=1)  32.7 us
    psum x3, blocking collectives, body(): lax.psum((misfit_local, count_local), 'bl')  29.6 us
    dot_general x8, matrix products, pick_stations(): jnp.dot(flat, table, precision=lax.Precision.HIGHEST, preferred_element_t...  20.6 us
  transfers between devices with their start and end apart: 4, of which 4 were waited for; matrix products, arithmetic and copies ran while one was open for 4% of the time, Pallas kernels for 0%

profile of v1, /device:TPU:8, one launch (start us, length us, event | category | flops | bytes accessed | tf_op | source)
XLA Modules:
  0.0 393.0 jit_solution(8092292597566114061)
XLA Ops:
  16.0 9.0 %fusion.102 = (f32[2,16,2048]{2,1,0:T(8,128)S(1)}, f32[2,16,2048]{2,1,0:T(8,128)S(1)}) fusion(f32[8,16,2048]{2,1,0:T(8,128)S(1)} %bitcast.263, f32[16]{0:T(128)S(1)} %copy-done.30, f32[8,2,2048]{2,1,0:T(2,128)S(1)} %add_multiply_fusion, f32[8,16]{1,0:T(8,128)S(1)} %copy-done.28, f32[8,16,2048]{2,1,0:T(8,128)S(1)} %bitcast.261), kind=kLoop, calls=%fused_computation.115 | loop fusion | flops 5636096 | bytes 2753088 | tf_op jit(solution)/shard_map/reduce_sum | solution.py:57
  27.2 10.5 %all-reduce.2 = (f32[]{:T(128)}, f32[]{:T(128)}) all-reduce(f32[]{:T(128)} %get-tuple-element.34, f32[]{:T(128)} %get-tuple-element.33), channel_id=1, replica_groups=mesh['bl'=4,'freq'=8] {'bl'}, use_global_device_ids=true, to_apply=%region_3.0 | all-reduce | flops 2 | bytes 16 | tf_op jit(solution)/shard_map/psum | solution.py:188
  37.7 11.8 %all-reduce.1 = (f32[]{:T(128)}, f32[]{:T(128)}) all-reduce(f32[]{:T(128)} %get-tuple-element.39, f32[]{:T(128)} %get-tuple-element.40), channel_id=1, replica_groups=mesh['bl'=4,'freq'=8] {'freq'}, use_global_device_ids=true, to_apply=%region_4.0 | all-reduce | flops 2 | bytes 16 | tf_op jit(solution)/shard_map/psum | solution.py:188
  51.9 10.9 %fusion.36 = (f32[8,16,2048]{2,1,0:T(8,128)S(1)}, f32[8,16,2048]{2,1,0:T(8,128)S(1)}, f32[8,16,2048]{2,1,0:T(8,128)S(1)}) fusion(f32[2,16,2048]{2,1,0:T(8,128)} %get-tuple-element.108, f32[2,16,2048]{2,1,0:T(8,128)S(1)} %get-tuple-element.107, f32[2,16,2048]{2,1,0:T(8,128)S(1)} %add_divide_fusion.2, f32[8,16,2048]{2,1,0:T(8,128)S(1)} %bitcast.264, ...), kind=kLoop, calls=%fused_computation.46 | loop fusion | flops 12845056 | bytes 6160960 | tf_op jit(solution)/shard_map/reduce_sum | solution.py:85
  68.2 3.9 fusion.103
  73.3 25.2 %reduce-scatter.4.cloned.1.call-done = f32[3,8,16,128]{3,2,1,0:T(8,128)} async-done(((f32[3,8,16,512]{3,2,1,0:T(8,128)}), f32[3,8,16,128]{3,2,1,0:T(8,128)}) %reduce-scatter.4.cloned.1.call-update) | async-done | bytes 196624 | tf_op jit(solution)/shard_map/reduce_scatter | solution.py:203
  99.5 13.2 %all_gather.9 = f32[2,8,16,512]{3,2,1,0:T(8,128)S(1)} all-gather(f32[2,8,16,128]{3,2,1,0:T(8,128)S(1)} %pad_maximum_fusion.7), channel_id=1, replica_groups=mesh['bl'=4,'freq'=8] {'bl'}, dimensions={3}, use_global_device_ids=true | all-gather | bytes 655360 | tf_op jit(solution)/shard_map/all_gather | solution.py:213
  119.4 8.9 %fusion.98 = (f32[2,16,2048]{2,1,0:T(8,128)S(1)}, f32[2,16,2048]{2,1,0:T(8,128)S(1)}) fusion(f32[8,16,2048]{2,1,0:T(8,128)S(1)} %bitcast.271, f32[8,16,2048]{2,1,0:T(8,128)S(1)} %bitcast.269, f32[16]{0:T(128)S(1)} %copy-done.30, f32[8,2,2048]{2,1,0:T(2,128)S(1)} %add_multiply_fusion, f32[8,16]{1,0:T(8,128)S(1)} %copy-done.28), kind=kLoop, calls=%fused_computation.111 | loop fusion | flops 5636096 | bytes 2753088 | tf_op jit(solution)/shard_map/reduce_sum | solution.py:57
  130.4 9.5 %psum.86 = f32[]{:T(128)} all-reduce(f32[]{:T(128)} %get-tuple-element.46), channel_id=1, replica_groups=mesh['bl'=4,'freq'=8] {'bl'}, use_global_device_ids=true, to_apply=%region_15.0 | all-reduce | flops 1 | bytes 8 | tf_op jit(solution)/shard_map/psum | solution.py:188
  141.7 11.0 %psum.87 = f32[]{:T(128)} all-reduce(f32[]{:T(128)} %psum.86), channel_id=1, replica_groups=mesh['bl'=4,'freq'=8] {'freq'}, use_global_device_ids=true, to_apply=%region_16.0 | all-reduce | flops 1 | bytes 8 | tf_op jit(solution)/shard_map/psum | solution.py:188
  154.4 10.9 %fusion.45 = (f32[8,16,2048]{2,1,0:T(8,128)S(1)}, f32[8,16,2048]{2,1,0:T(8,128)S(1)}, f32[8,16,2048]{2,1,0:T(8,128)S(1)}) fusion(f32[2,16,2048]{2,1,0:T(8,128)} %get-tuple-element.102, f32[2,16,2048]{2,1,0:T(8,128)} %get-tuple-element.101, f32[2,16,2048]{2,1,0:T(8,128)S(1)} %add_divide_fusion.1, f32[8,16,2048]{2,1,0:T(8,128)S(1)} %bitcast.272, ...), kind=kLoop, calls=%fused_computation.55 | loop fusion | flops 12845056 | bytes 6160960 | tf_op jit(solution)/shard_map/reduce_sum | solution.py:85
  170.4 3.9 fusion.104
  174.7 25.8 %reduce-scatter.6.cloned.1.call-done = f32[3,8,16,128]{3,2,1,0:T(8,128)} async-done(((f32[3,8,16,512]{3,2,1,0:T(8,128)}), f32[3,8,16,128]{3,2,1,0:T(8,128)}) %reduce-scatter.6.cloned.1.call-update) | async-done | bytes 196624 | tf_op jit(solution)/shard_map/reduce_scatter | solution.py:203
  201.6 13.5 %all_gather.10 = f32[2,8,16,512]{3,2,1,0:T(8,128)S(1)} all-gather(f32[2,8,16,128]{3,2,1,0:T(8,128)S(1)} %pad_maximum_fusion.8), channel_id=1, replica_groups=mesh['bl'=4,'freq'=8] {'bl'}, dimensions={3}, use_global_device_ids=true | all-gather | bytes 655360 | tf_op jit(solution)/shard_map/all_gather | solution.py:213
  221.7 8.9 %fusion.94 = (f32[2,16,2048]{2,1,0:T(8,128)S(1)}, f32[2,16,2048]{2,1,0:T(8,128)S(1)}) fusion(f32[8,16,2048]{2,1,0:T(8,128)S(1)} %bitcast.267, f32[8,16,2048]{2,1,0:T(8,128)S(1)} %bitcast.265, f32[16]{0:T(128)S(1)} %copy-done.30, f32[8,2,2048]{2,1,0:T(2,128)S(1)} %add_multiply_fusion, f32[8,16]{1,0:T(8,128)S(1)} %copy-done.28), kind=kLoop, calls=%fused_computation.107 | loop fusion | flops 5636096 | bytes 2753088 | tf_op jit(solution)/shard_map/reduce_sum | solution.py:57
  232.8 9.5 %psum.88 = f32[]{:T(128)} all-reduce(f32[]{:T(128)} %get-tuple-element.44), channel_id=1, replica_groups=mesh['bl'=4,'freq'=8] {'bl'}, use_global_device_ids=true, to_apply=%region_24.0 | all-reduce | flops 1 | bytes 8 | tf_op jit(solution)/shard_map/psum | solution.py:188
  244.1 10.8 %all-reduce = (f32[]{:T(128)}, f32[3,3]{0,1:T(4,128)S(1)}) all-reduce(f32[]{:T(128)} %psum.88, f32[3,3]{0,1:T(4,128)S(1)} %fusion.163), channel_id=1, replica_groups=mesh['bl'=4,'freq'=8] {'freq'}, use_global_device_ids=true, to_apply=%region_25.0 | all-reduce | flops 10 | bytes 80 | tf_op jit(solution)/shard_map/psum | solution.py:188
  256.6 10.9 %fusion.53 = (f32[8,16,2048]{2,1,0:T(8,128)S(1)}, f32[8,16,2048]{2,1,0:T(8,128)S(1)}, f32[8,16,2048]{2,1,0:T(8,128)S(1)}) fusion(f32[2,16,2048]{2,1,0:T(8,128)} %get-tuple-element.98, f32[2,16,2048]{2,1,0:T(8,128)} %get-tuple-element.97, f32[2,16,2048]{2,1,0:T(8,128)S(1)} %add_divide_fusion, f32[8,16,2048]{2,1,0:T(8,128)S(1)} %bitcast.268, ...), kind=kLoop, calls=%fused_computation.63 | loop fusion | flops 12845056 | bytes 6160960 | tf_op jit(solution)/shard_map/reduce_sum | solution.py:85
  272.6 3.9 fusion.105
  280.4 22.4 %reduce-scatter.8.cloned.1.call-done = f32[3,8,16,128]{3,2,1,0:T(8,128)} async-done(((f32[3,8,16,512]{3,2,1,0:T(8,128)}), f32[3,8,16,128]{3,2,1,0:T(8,128)}) %reduce-scatter.8.cloned.1.call-update) | async-done | bytes 196624 | tf_op jit(solution)/shard_map/reduce_scatter | solution.py:203
  303.9 13.3 %all_gather.11 = f32[2,8,16,512]{3,2,1,0:T(8,128)S(1)} all-gather(f32[2,8,16,128]{3,2,1,0:T(8,128)S(1)} %pad_maximum_fusion.9), channel_id=1, replica_groups=mesh['bl'=4,'freq'=8] {'bl'}, dimensions={3}, use_global_device_ids=true | all-gather | bytes 655360 | tf_op jit(solution)/shard_map/all_gather | solution.py:213
  327.7 8.9 %fusion.58 = (f32[2,16,2048]{2,1,0:T(8,128)S(1)}, f32[2,16,2048]{2,1,0:T(8,128)S(1)}) fusion(f32[8,16,2048]{2,1,0:T(8,128)S(1)} %bitcast.276, f32[8,16,2048]{2,1,0:T(8,128)S(1)} %bitcast.275, f32[16]{0:T(128)S(1)} %copy-done.30, f32[8,2,2048]{2,1,0:T(2,128)S(1)} %add_multiply_fusion, f32[8,16]{1,0:T(8,128)S(1)} %copy-done.28), kind=kLoop, calls=%fused_computation.68 | loop fusion | flops 5636096 | bytes 2753088 | tf_op jit(solution)/shard_map/reduce_sum | solution.py:57
  337.6 41.7 %all-reduce.5.cloned.1.call-done = f32[3,2,8,512]{3,2,1,0:T(8,128)} async-done(((f32[3,2,8,512]{3,2,1,0:T(8,128)}), f32[3,2,8,512]{3,2,1,0:T(8,128)}) %all-reduce.5.cloned.1.call-update) | async-done | bytes 98320 | tf_op jit(solution)/shard_map/psum | solution.py:224
  379.3 4.0 %subtract_divide_fusion = (f32[1,2,8,512]{3,2,1,0:T(8,128)S(1)}, f32[1,2,8,512]{3,2,1,0:T(8,128)S(1)}, f32[1,2,8,512]{3,2,1,0:T(8,128)S(1)}) fusion(f32[]{:T(128)} %bitcast.72, f32[]{:T(128)} %bitcast.69, f32[]{:T(128)} %bitcast.68, f32[3,2,8,512]{3,2,1,0:T(8,128)} %all-reduce.5.cloned.1.call-done, f32[]{:T(128)} %bitcast.71, f32[]{:T(128)} %bitcast.70, ...), kind=kLoop, calls=%fused_computation.253 | loop fusion | flops 139264 | bytes 196632 | tf_op jit(solution)/shard_map/div | solution.py:139
  (140 shorter events, 71.7 us)
Async XLA Ops:
  7.2 65.1 %copy-start = (f32[2,3,8,512]{3,2,1,0:T(8,128)S(1)}, f32[2,3,8,512]{3,2,1,0:T(8,128)}, u32[]{:S(2)}) copy-start(f32[2,3,8,512]{3,2,1,0:T(8,128)} %param.20) | copy-start | bytes 294916
  7.2 91.3 %reduce-scatter.4.cloned.1.call-start = ((), (), s32[]{:S(2)}) async-start(), calls=%async_computation.3 | async-start | bytes 983040 | tf_op jit(solution)/shard_map/reduce_scatter | solution.py:203
  15.8 9.2 %copy-start.2 = (f32[2,2,16,2048]{3,2,1,0:T(8,128)S(1)}, f32[2,2,16,2048]{3,2,1,0:T(8,128)}, u32[]{:S(2)}) copy-start(f32[2,2,16,2048]{3,2,1,0:T(8,128)} %param.11) | copy-start | bytes 1572868
  16.0 9.8 %copy-start.3 = (s32[2,16,2048]{2,1,0:T(8,128)S(1)}, s32[2,16,2048]{2,1,0:T(8,128)}, u32[]{:S(2)}) copy-start(s32[2,16,2048]{2,1,0:T(8,128)} %param.12) | copy-start | bytes 786436
  51.9 10.9 %copy-start.4 = (f32[128,2048]{1,0:T(8,128)S(1)}, f32[128,2048]{1,0:T(8,128)}, u32[]{:S(2)}) copy-start(f32[128,2048]{1,0:T(8,128)} %get-tuple-element.89) | copy-start | bytes 3145732
  51.9 10.9 %copy-start.5 = (f32[128,2048]{1,0:T(8,128)S(1)}, f32[128,2048]{1,0:T(8,128)}, u32[]{:S(2)}) copy-start(f32[128,2048]{1,0:T(8,128)} %get-tuple-element.90) | copy-start | bytes 3145732
  51.9 10.9 %copy-start.6 = (f32[128,2048]{1,0:T(8,128)S(1)}, f32[128,2048]{1,0:T(8,128)}, u32[]{:S(2)}) copy-start(f32[128,2048]{1,0:T(8,128)} %get-tuple-element.91) | copy-start | bytes 3145732
  51.9 10.9 %copy-start.7 = (f32[128,2048]{1,0:T(8,128)S(1)}, f32[128,2048]{1,0:T(8,128)}, u32[]{:S(2)}) copy-start(f32[128,2048]{1,0:T(8,128)} %get-tuple-element.92) | copy-start | bytes 3145732
  72.2 128.4 %reduce-scatter.6.cloned.1.call-start = ((), (), s32[]{:S(2)}) async-start(), calls=%async_computation.4 | async-start | bytes 983040 | tf_op jit(solution)/shard_map/reduce_scatter | solution.py:203
  73.3 41.6 %copy-start.24 = (f32[1,8,16,512]{3,2,1,0:T(8,128)}, f32[1,8,16,512]{3,2,1,0:T(8,128)S(1)}, u32[]{:S(2)}) copy-start(f32[1,8,16,512]{3,2,1,0:T(8,128)S(1)} %get-tuple-element.103) | copy-start | bytes 786436
  73.3 41.6 %copy-start.25 = (f32[1,8,16,512]{3,2,1,0:T(8,128)}, f32[1,8,16,512]{3,2,1,0:T(8,128)S(1)}, u32[]{:S(2)}) copy-start(f32[1,8,16,512]{3,2,1,0:T(8,128)S(1)} %get-tuple-element.104) | copy-start | bytes 786436
  154.4 11.0 %copy-start.12 = (f32[128,2048]{1,0:T(8,128)S(1)}, f32[128,2048]{1,0:T(8,128)}, u32[]{:S(2)}) copy-start(f32[128,2048]{1,0:T(8,128)} %get-tuple-element.81) | copy-start | bytes 3145732
  154.4 11.0 %copy-start.13 = (f32[128,2048]{1,0:T(8,128)S(1)}, f32[128,2048]{1,0:T(8,128)}, u32[]{:S(2)}) copy-start(f32[128,2048]{1,0:T(8,128)} %get-tuple-element.82) | copy-start | bytes 3145732
  154.4 11.0 %copy-start.14 = (f32[128,2048]{1,0:T(8,128)S(1)}, f32[128,2048]{1,0:T(8,128)}, u32[]{:S(2)}) copy-start(f32[128,2048]{1,0:T(8,128)} %get-tuple-element.83) | copy-start | bytes 3145732
  154.4 11.0 %copy-start.15 = (f32[128,2048]{1,0:T(8,128)S(1)}, f32[128,2048]{1,0:T(8,128)}, u32[]{:S(2)}) copy-start(f32[128,2048]{1,0:T(8,128)} %get-tuple-element.84) | copy-start | bytes 3145732
  170.4 4.2 %copy-start.23 = (f32[2,8,16,512]{3,2,1,0:T(8,128)S(1)}, f32[2,8,16,512]{3,2,1,0:T(8,128)}, u32[]{:S(2)}) copy-start(f32[2,8,16,512]{3,2,1,0:T(8,128)} %copy-done.22) | copy-start | bytes 1572868
  174.4 128.4 %reduce-scatter.8.cloned.1.call-start = ((), (), s32[]{:S(2)}) async-start(), calls=%async_computation.5 | async-start | bytes 983040 | tf_op jit(solution)/shard_map/reduce_scatter | solution.py:203
  256.6 11.0 %copy-start.8 = (f32[128,2048]{1,0:T(8,128)S(1)}, f32[128,2048]{1,0:T(8,128)}, u32[]{:S(2)}) copy-start(f32[128,2048]{1,0:T(8,128)} %get-tuple-element.73) | copy-start | bytes 3145732
  256.6 11.0 %copy-start.9 = (f32[128,2048]{1,0:T(8,128)S(1)}, f32[128,2048]{1,0:T(8,128)}, u32[]{:S(2)}) copy-start(f32[128,2048]{1,0:T(8,128)} %get-tuple-element.74) | copy-start | bytes 3145732
  256.6 11.0 %copy-start.10 = (f32[128,2048]{1,0:T(8,128)S(1)}, f32[128,2048]{1,0:T(8,128)}, u32[]{:S(2)}) copy-start(f32[128,2048]{1,0:T(8,128)} %get-tuple-element.75) | copy-start | bytes 3145732
  256.6 11.0 %copy-start.11 = (f32[128,2048]{1,0:T(8,128)S(1)}, f32[128,2048]{1,0:T(8,128)}, u32[]{:S(2)}) copy-start(f32[128,2048]{1,0:T(8,128)} %get-tuple-element.76) | copy-start | bytes 3145732
  272.6 7.7 %copy-start.21 = (f32[2,8,16,512]{3,2,1,0:T(8,128)S(1)}, f32[2,8,16,512]{3,2,1,0:T(8,128)}, u32[]{:S(2)}) copy-start(f32[2,8,16,512]{3,2,1,0:T(8,128)} %copy-done.20) | copy-start | bytes 1572868
  276.6 102.7 %all-reduce.5.cloned.1.call-start = ((), (), s32[]{:S(2)}) async-start(), calls=%async_computation.6 | async-start | bytes 196608 | tf_op jit(solution)/shard_map/psum | solution.py:224
  336.7 49.6 %copy-start.1 = (f32[2,3,8,512]{3,2,1,0:T(8,128)S(1)}, f32[2,3,8,512]{3,2,1,0:T(8,128)}, u32[]{:S(2)}) copy-start(f32[2,3,8,512]{3,2,1,0:T(8,128)} %param.20) | copy-start | bytes 294916
  (13 other events, 30.9 us)
Sparse Core Ops, SparseCore 0:
  72.3 26.1 reduce-scatter.3
  174.5 25.9 reduce-scatter.5
  276.7 26.0 reduce-scatter.7
  325.3 53.9 all-reduce.4
